TPU v7x, 512 devices: a whole 4x4x16 slice. The times are simulated.
512 devices in a mesh: leaf: 128 (over z, y, core), rep: 4 (over x).
Axes of the slice: x: 4, y: 4, z: 16, core: 2. Of those that a mesh axis runs over, the one named last changes fastest.
Arguments:
- positions: float32 [3, 8192, 128], P(None, ('leaf', 'rep')), may hold values from -6 to 6
- density: float32 [3, 8192, 128], P(None, ('leaf', 'rep')), may hold values from -6 to 6
- near_offset: int32 [8192, 12], P(('leaf', 'rep')), may hold values from -2 to 2
- near_count: int32 [8192], P(('leaf', 'rep')), may hold values from 1 to 12
- inter_list: int32 [512, 189], P(('leaf', 'rep')), may hold values from 0 to 511
- operator_index: int32 [512, 189], P(('leaf', 'rep')), may hold values from 0 to 3
- lattice_index: int32 [512], P(('leaf', 'rep')), may hold values from 0 to 1
- up_weight: bfloat16 [512, 384], replicated, may hold values from -0.3125 to 0.3125
- m2l_operators: bfloat16 [4, 512, 512], replicated, may hold values from -0.0390625 to 0.0390625
- lattice_operators: bfloat16 [2, 512, 512], replicated, may hold values from -0.01171875 to 0.01171875
- down_weight: bfloat16 [384, 512], replicated, may hold values from -0.5 to 0.5
Outputs:
- velocity: float32 [3, 8192, 128], P(None, ('leaf', 'rep'))
Inputs may be any that keep to these rules, and one draw needn't show every extreme that they name: `near_offset`: leaf g's near source leaves are (g + offset) mod 8192; slots at or past near_count are unused.
All inputs are finite; a program needn't handle non-finite values.
Results may differ from a plain program's by a relative error of at most 0.02.
Values may be sent and summed in bfloat16 or wider, within the bound.
A program may use at most 64 MiB of HBM per device.

v0:
```python
import math
import jax
import jax.numpy as jnp
from jax import lax
from jax.sharding import PartitionSpec as P


def padded(shard, sides, width):
    for axis, dim in sides:
        size, length = (lax.axis_size(axis), shard.shape[dim])
        up = [(i, (i + 1) % size) for i in range(size)]
        down = [(j, i) for i, j in up]
        last = lax.slice_in_dim(shard, length - width, length, axis=dim)
        first = lax.slice_in_dim(shard, 0, width, axis=dim)
        before = lax.ppermute(last, axis, up)
        after = lax.ppermute(first, axis, down)
        shard = jnp.concatenate([before, shard, after], axis=dim)
    return shard


def stokes_tile(target, source_pos, source_force, live_slots):
    offsets_xyz = target[:, None, :, None] - source_pos[:, :, None, :]
    distance_sq = jnp.sum(offsets_xyz * offsets_xyz, axis=0) + 0.05
    inverse = lax.rsqrt(distance_sq)
    inverse_cube = inverse * inverse * inverse
    projected = jnp.sum(offsets_xyz * source_force[:, :, None, :], axis=0)
    kernel_terms = source_force[:, :, None, :] * inverse + offsets_xyz * (projected * inverse_cube)
    kernel_terms = kernel_terms * live_slots[None, :, None, None]
    return jnp.sum(kernel_terms, axis=(1, 3)) * (1.0 / (8.0 * math.pi))


def body(
    positions,
    density,
    near_offset,
    near_count,
    inter_list,
    operator_index,
    lattice_index,
    up_weight,
    m2l_operators,
    lattice_operators,
    down_weight,
):
    per_box = positions.shape[1]
    node_count = positions.shape[2]
    kind_count = m2l_operators.shape[0]
    stacked = jnp.concatenate([positions, density], axis=0)
    extended = padded(stacked.astype(jnp.bfloat16), ((("leaf", "rep"), 1),), per_box).astype(
        stacked.dtype
    )
    slot_range = jnp.arange(near_offset.shape[1], dtype=jnp.int32)

    def one_leaf(leaf_slot):
        target = positions[:, leaf_slot]
        source_slot = leaf_slot + near_offset[leaf_slot] + per_box
        sources = jnp.take(extended, source_slot, axis=1)
        live_slots = (slot_range < near_count[leaf_slot]).astype(jnp.float32)
        return stokes_tile(target, sources[:3], sources[3:], live_slots)

    near_part = lax.map(one_leaf, jnp.arange(per_box, dtype=jnp.int32))
    near_part = jnp.transpose(near_part, (1, 0, 2))
    damping = 1.0 / (1.0 + jnp.sum(positions * positions, axis=0))
    summed = jnp.sum(density * damping[None], axis=1).reshape(-1).astype(jnp.bfloat16)
    coarse = jnp.dot(up_weight, summed, preferred_element_type=jnp.float32).astype(jnp.bfloat16)
    coarse_row = coarse.reshape(1, -1)
    box_ids = inter_list[0]
    op_kinds = operator_index[0]
    kind_range = jnp.arange(kind_count, dtype=jnp.int32)
    selector = (op_kinds[None, :] == kind_range[:, None]).astype(jnp.float32)
    all_blocks = lax.all_gather(coarse_row, ("leaf", "rep"), axis=0, tiled=True)
    chosen = jnp.take(all_blocks, box_ids, axis=0).astype(jnp.float32)
    grouped_sum = jnp.dot(selector, chosen, precision=lax.Precision.HIGHEST)
    block_sum = jnp.sum(all_blocks.astype(jnp.float32), axis=0)
    block_sum = lax.psum(coarse.astype(jnp.float32), ("leaf", "rep"))
    total = block_sum.astype(jnp.bfloat16)
    grouped = grouped_sum.astype(jnp.bfloat16)
    local = jnp.einsum("tij,tj->i", m2l_operators, grouped, preferred_element_type=jnp.float32)
    local = local + jnp.dot(
        lattice_operators[lattice_index[0]], total, preferred_element_type=jnp.float32
    )
    local_bf = local.astype(jnp.bfloat16)
    far_part = jnp.dot(down_weight, local_bf, preferred_element_type=jnp.float32).reshape(
        3, node_count
    )
    return near_part + damping[None] * far_part[:, None, :]


def solution(mesh):
    in_specs = (
        P(None, ("leaf", "rep"), None),
        P(None, ("leaf", "rep"), None),
        P(("leaf", "rep"), None),
        P(("leaf", "rep")),
        P(("leaf", "rep"), None),
        P(("leaf", "rep"), None),
        P(("leaf", "rep")),
        P(),
        P(),
        P(),
        P(),
    )
    out_specs = P(None, ("leaf", "rep"), None)
    return jax.shard_map(body, mesh=mesh, in_specs=in_specs, out_specs=out_specs, check_vma=False)
```

profile of v0, /device:TPU:4, one launch (start us, length us, event | category | flops | bytes accessed | tf_op | source)
XLA Modules:
  0.0 417.0 jit_solution(9846070013614672958)
XLA Ops:
  1.8 3.1 collective-permute-start
  4.9 2.7 collective-permute-start.1
  8.9 108.3 %psum.7 = bf16[512]{0:T(512)(128)(2,1)S(1)} all-reduce(bf16[512]{0:T(512)(128)(2,1)S(1)} %convert_element_type.40), channel_id=1, replica_groups=mesh['leaf'=128,'rep'=4] {'leaf','rep'}, use_global_device_ids=true, to_apply=%region_7.8 | all-reduce | flops 512 | bytes 2048 | tf_op jit(solution)/shard_map/psum | solution.py:75
  117.8 136.1 %all-gather.1 = bf16[512,1,512]{2,1,0:T(2,128)(2,1)S(1)} all-gather(bf16[1,1,512]{2,1,0:T(2,128)(2,1)S(1)} %reshape.142), channel_id=2, replica_groups=mesh['leaf'=128,'rep'=4] {'leaf','rep'}, dimensions={0}, use_global_device_ids=true | all-gather | bytes 525312 | tf_op jit(solution)/shard_map/all_gather | solution.py:71
  257.8 158.6 %while.13 = (s32[]{:T(128)}, f32[16,3,128]{2,0,1:T(8,128)S(1)}, s32[16]{0:T(128)S(1)}, s32[16,12]{1,0:T(8,128)}, f32[6,48,128]{2,0,1:T(8,128)S(1)}, /*index=5*/f...) while((s32[]{:T(128)}, f32[16,3,128]{2,0,1:T(8,128)S(1)}, ...), condition=%wide.region_4.5_spmd.clone, body=%wide.region_0.4_spmd.clone.sunk | while | flops 6891705 | bytes 6684707 | solution.py:61
  260.5 1.4 fusion.33
  262.5 1.4 compare_and_fusion.3
  270.4 1.4 fusion.33
  272.4 1.4 compare_and_fusion.3
  280.3 1.4 fusion.33
  282.3 1.4 compare_and_fusion.3
  290.3 1.4 fusion.33
  292.2 1.4 compare_and_fusion.3
  300.2 1.4 fusion.33
  302.1 1.4 compare_and_fusion.3
  310.1 1.4 fusion.33
  312.0 1.4 compare_and_fusion.3
  320.0 1.4 fusion.33
  322.0 1.4 compare_and_fusion.3
  329.9 1.4 fusion.33
  331.9 1.4 compare_and_fusion.3
  339.8 1.4 fusion.33
  341.8 1.4 compare_and_fusion.3
  349.7 1.4 fusion.33
  351.7 1.4 compare_and_fusion.3
  359.6 1.4 fusion.33
  361.6 1.4 compare_and_fusion.3
  371.5 1.4 compare_and_fusion.3
  381.4 1.4 compare_and_fusion.3
  391.3 1.4 compare_and_fusion.3
  401.3 1.4 compare_and_fusion.3
  411.2 1.4 compare_and_fusion.3
  (314 shorter events, 93.6 us)
Async XLA Ops:
  0.0 255.4 %copy-start = (bf16[4,512,512]{2,1,0:T(8,128)(2,1)S(1)}, bf16[4,512,512]{2,1,0:T(8,128)(2,1)}, u32[]{:S(2)}) copy-start(bf16[4,512,512]{2,1,0:T(8,128)(2,1)} %param.21) | copy-start | bytes 6291460
  0.0 254.1 %copy-start.2 = (s32[1,189]{1,0:T(1,128)S(1)}, s32[1,189]{1,0:T(1,128)}, u32[]{:S(2)}) copy-start(s32[1,189]{1,0:T(1,128)} %param.17) | copy-start | bytes 2272
  1.8 255.9 %collective-permute-start = (bf16[6,16,128]{2,1,0:T(8,128)(2,1)S(1)}, bf16[6,16,128]{2,1,0:T(8,128)(2,1)S(1)}, u32[]{:S(2)}, u32[]{:S(2)}) collective-permute-start(bf16[6,16,128]{2,1,0:T(8,128)(2,1)S(1)} %pad_maximum_fusion), channel_id=1, source_target_pairs={{0,1},{1,2},{2,3},{3,4},{4,5},{5,6},{6,7},{7,8},{8,9},{9,10},{10,1... | collective-permute-start | bytes 73736 | tf_op jit(solution)/shard_map/ppermute | solution.py:15
  4.9 252.8 %collective-permute-start.1 = (bf16[6,16,128]{2,1,0:T(8,128)(2,1)S(1)}, bf16[6,16,128]{2,1,0:T(8,128)(2,1)S(1)}, u32[]{:S(2)}, u32[]{:S(2)}) collective-permute-start(bf16[6,16,128]{2,1,0:T(8,128)(2,1)S(1)} %pad_maximum_fusion), channel_id=1, source_target_pairs={{1,0},{2,1},{3,2},{4,3},{5,4},{6,5},{7,6},{8,7},{9,8},{10,9},{11,1... | collective-permute-start | bytes 73736 | tf_op jit(solution)/shard_map/ppermute | solution.py:16
  117.8 137.4 %copy-start.3 = (s32[1,189]{1,0:T(1,128)S(1)}, s32[1,189]{1,0:T(1,128)}, u32[]{:S(2)}) copy-start(s32[1,189]{1,0:T(1,128)} %param.18) | copy-start | bytes 2272
  254.1 3.2 copy-start.1
  255.2 2.6 copy-start.4
where the time goes:
time: 420 us; the launch traced here: 417 us
  blocking collectives  244 us (58%)
  other arithmetic  83.3 us (20%)
  local copies, waits for them, and re-layouts  44.2 us (11%)
  loops' own time  34.7 us (8%)
  starting transfers between devices  5.84 us (1%)
    all_gather x1, blocking collectives, body(): all_blocks = lax.all_gather(coarse_row, ('leaf', 'rep'), axis=0, tiled=True)  136 us
    psum x1, blocking collectives, body(): block_sum = lax.psum(coarse.astype(jnp.float32), ('leaf', 'rep'))  108 us
    another operation x1, loops' own time, body(): near_part = lax.map(one_leaf, jnp.arange(per_box, dtype=jnp.int32))  34.7 us
    select_n x32, other arithmetic, one_leaf(): sources = jnp.take(extended, source_slot, axis=1)  23.5 us
    and x16, other arithmetic, one_leaf(): sources = jnp.take(extended, source_slot, axis=1)  22.2 us
    dynamic_slice x32, local copies, waits for them, and re-layouts, one_leaf(): target = positions[:, leaf_slot]  11.6 us
    convert_element_type x16, other arithmetic, one_leaf(): live_slots = (slot_range < near_count[leaf_slot]).astype(jnp.float32)  11 us
    reduce_sum x16, other arithmetic, stokes_tile(): return jnp.sum(kernel_terms, axis=(1, 3)) * (1.0 / (8.0 * math.pi))  10.7 us
  transfers between devices with their start and end apart: 2, of which 0 were waited for; matrix products, arithmetic and copies ran while one was open for 1% of the time, Pallas kernels for 0%

commit v1 on v0

--- a/solution.py
+++ b/solution.py
@@ -72,7 +72,7 @@
     chosen = jnp.take(all_blocks, box_ids, axis=0).astype(jnp.float32)
     grouped_sum = jnp.dot(selector, chosen, precision=lax.Precision.HIGHEST)
     block_sum = jnp.sum(all_blocks.astype(jnp.float32), axis=0)
-    block_sum = lax.psum(coarse.astype(jnp.float32), ("leaf", "rep"))
+    block_sum = jnp.sum(lax.all_gather(coarse.astype(jnp.float32), ("leaf", "rep")), axis=0)
     total = block_sum.astype(jnp.bfloat16)
     grouped = grouped_sum.astype(jnp.bfloat16)
     local = jnp.einsum("tij,tj->i", m2l_operators, grouped, preferred_element_type=jnp.float32)

time: 420 us -> 322 us (0.77)
  the two profiles are of different devices: /device:TPU:4 before, /device:TPU:2 now
where the time goes in v1:
time: 322 us; the launch traced here: 319 us
  blocking collectives  142 us (44%)
  other arithmetic  79.5 us (25%)
  local copies, waits for them, and re-layouts  41.7 us (13%)
  loops' own time  28.5 us (9%)
  between operations  14.3 us (4%)
  starting transfers between devices  9.74 us (3%)
  matrix products  3.57 us (1%)
    all_gather x1, blocking collectives, body(): all_blocks = lax.all_gather(coarse_row, ('leaf', 'rep'), axis=0, tiled=True)  142 us
    another operation x1, loops' own time, body(): near_part = lax.map(one_leaf, jnp.arange(per_box, dtype=jnp.int32))  28.5 us
    select_n x32, other arithmetic, one_leaf(): sources = jnp.take(extended, source_slot, axis=1)  21.4 us
    and x16, other arithmetic, one_leaf(): sources = jnp.take(extended, source_slot, axis=1)  20.2 us
    dynamic_slice x32, local copies, waits for them, and re-layouts, one_leaf(): target = positions[:, leaf_slot]  11.6 us
    reduce_sum x16, other arithmetic, stokes_tile(): return jnp.sum(kernel_terms, axis=(1, 3)) * (1.0 / (8.0 * math.pi))  10.7 us
    reduce_sum x16, other arithmetic, stokes_tile(): distance_sq = jnp.sum(offsets_xyz * offsets_xyz, axis=0) + 0.05  10.2 us
    dynamic_slice x16, local copies, waits for them, and re-layouts, one_leaf(): live_slots = (slot_range < near_count[leaf_slot]).astype(jnp.float32)  9.42 us
  transfers between devices with their start and end apart: 3, of which 0 were waited for; matrix products, arithmetic and copies ran while one was open for 37% of the time, Pallas kernels for 0%

profile of v1, /device:TPU:2, one launch (start us, length us, event | category | flops | bytes accessed | tf_op | source)
XLA Modules:
  0.0 319.1 jit_solution(14168430391813079792)
XLA Ops:
  8.3 3.4 %collective-permute-start = (bf16[6,16,128]{2,1,0:T(8,128)(2,1)S(1)}, bf16[6,16,128]{2,1,0:T(8,128)(2,1)S(1)}, u32[]{:S(2)}, u32[]{:S(2)}) collective-permute-start(bf16[6,16,128]{2,1,0:T(8,128)(2,1)S(1)} %pad_maximum_fusion), channel_id=1, source_target_pairs={{0,1},{1,2},{2,3},{3,4},{4,5},{5,6},{6,7},{7,8},{8,9},{9,10},{10,1... | collective-permute-start | bytes 73736 | tf_op jit(solution)/shard_map/ppermute | solution.py:15
  11.7 6.3 %collective-permute-start.1 = (bf16[6,16,128]{2,1,0:T(8,128)(2,1)S(1)}, bf16[6,16,128]{2,1,0:T(8,128)(2,1)S(1)}, u32[]{:S(2)}, u32[]{:S(2)}) collective-permute-start(bf16[6,16,128]{2,1,0:T(8,128)(2,1)S(1)} %pad_maximum_fusion), channel_id=1, source_target_pairs={{1,0},{2,1},{3,2},{4,3},{5,4},{6,5},{7,6},{8,7},{9,8},{10,9},{11,1... | collective-permute-start | bytes 73736 | tf_op jit(solution)/shard_map/ppermute | solution.py:16
  19.9 141.8 %all-gather.2 = bf16[512,1,512]{2,1,0:T(2,128)(2,1)S(1)} all-gather(bf16[1,1,512]{2,1,0:T(2,128)(2,1)S(1)} %reshape.144), channel_id=2, replica_groups=mesh['leaf'=128,'rep'=4] {'leaf','rep'}, dimensions={0}, use_global_device_ids=true | all-gather | bytes 525312 | tf_op jit(solution)/shard_map/all_gather | solution.py:71
  164.6 143.5 %while.13 = (s32[]{:T(128)}, f32[16,3,128]{2,0,1:T(8,128)S(1)}, s32[16]{0:T(128)S(1)}, s32[16,12]{1,0:T(8,128)}, f32[6,48,128]{2,0,1:T(8,128)S(1)}, /*index=5*/f...) while((s32[]{:T(128)}, f32[16,3,128]{2,0,1:T(8,128)S(1)}, ...), condition=%wide.region_4.5_spmd.clone, body=%wide.region_0.4_spmd.clone.sunk | while | flops 6891705 | bytes 6684707 | solution.py:61
  166.9 1.3 fusion.34
  168.7 1.3 compare_and_fusion.3
  175.9 1.3 fusion.34
  177.7 1.3 compare_and_fusion.3
  184.8 1.3 fusion.34
  186.7 1.3 compare_and_fusion.3
  193.8 1.3 fusion.34
  195.6 1.3 compare_and_fusion.3
  202.8 1.3 fusion.34
  204.6 1.3 compare_and_fusion.3
  211.8 1.3 fusion.34
  213.6 1.3 compare_and_fusion.3
  222.6 1.3 compare_and_fusion.3
  229.7 1.3 fusion.34
  231.5 1.3 compare_and_fusion.3
  238.7 1.3 fusion.34
  240.5 1.3 compare_and_fusion.3
  249.5 1.3 compare_and_fusion.3
  256.6 1.3 fusion.34
  258.4 1.3 compare_and_fusion.3
  265.6 1.3 fusion.34
  267.4 1.3 compare_and_fusion.3
  276.4 1.3 compare_and_fusion.3
  285.3 1.3 compare_and_fusion.3
  294.3 1.3 compare_and_fusion.3
  303.3 1.3 compare_and_fusion.3
  308.2 1.8 reduce_sum.65
  310.0 1.3 fusion.10
  (317 shorter events, 88.9 us)
Async XLA Ops:
  6.5 156.6 %copy-start = (bf16[4,512,512]{2,1,0:T(8,128)(2,1)S(1)}, bf16[4,512,512]{2,1,0:T(8,128)(2,1)}, u32[]{:S(2)}) copy-start(bf16[4,512,512]{2,1,0:T(8,128)(2,1)} %param.21) | copy-start | bytes 6291460
  6.5 155.4 %copy-start.2 = (s32[1,189]{1,0:T(1,128)S(1)}, s32[1,189]{1,0:T(1,128)}, u32[]{:S(2)}) copy-start(s32[1,189]{1,0:T(1,128)} %param.17) | copy-start | bytes 2272
  6.5 301.6 %all-gather.6.cloned.1.call-start = ((), (), s32[]{:S(2)}) async-start(), calls=%async_computation | async-start | bytes 1050624 | tf_op jit(solution)/shard_map/all_gather | solution.py:75
  8.3 156.2 %collective-permute-start = (bf16[6,16,128]{2,1,0:T(8,128)(2,1)S(1)}, bf16[6,16,128]{2,1,0:T(8,128)(2,1)S(1)}, u32[]{:S(2)}, u32[]{:S(2)}) collective-permute-start(bf16[6,16,128]{2,1,0:T(8,128)(2,1)S(1)} %pad_maximum_fusion), channel_id=1, source_target_pairs={{0,1},{1,2},{2,3},{3,4},{4,5},{5,6},{6,7},{7,8},{8,9},{9,10},{10,1... | collective-permute-start | bytes 73736 | tf_op jit(solution)/shard_map/ppermute | solution.py:15
  11.7 152.8 %collective-permute-start.1 = (bf16[6,16,128]{2,1,0:T(8,128)(2,1)S(1)}, bf16[6,16,128]{2,1,0:T(8,128)(2,1)S(1)}, u32[]{:S(2)}, u32[]{:S(2)}) collective-permute-start(bf16[6,16,128]{2,1,0:T(8,128)(2,1)S(1)} %pad_maximum_fusion), channel_id=1, source_target_pairs={{1,0},{2,1},{3,2},{4,3},{5,4},{6,5},{7,6},{8,7},{9,8},{10,9},{11,1... | collective-permute-start | bytes 73736 | tf_op jit(solution)/shard_map/ppermute | solution.py:16
  19.9 143.0 %copy-start.3 = (s32[1,189]{1,0:T(1,128)S(1)}, s32[1,189]{1,0:T(1,128)}, u32[]{:S(2)}) copy-start(s32[1,189]{1,0:T(1,128)} %param.18) | copy-start | bytes 2272
  161.9 2.7 copy-start.4
  164.6 146.7 %copy-start.1 = (bf16[384,512]{1,0:T(8,128)(2,1)S(1)}, bf16[384,512]{1,0:T(8,128)(2,1)}, u32[]{:S(2)}) copy-start(bf16[384,512]{1,0:T(8,128)(2,1)} %param.23) | copy-start | bytes 1179652
Sparse Core Ops, SparseCore 0:
  20.0 168.4 all-gather.5
